TPU v7x, 32 devices: a whole 2x2x4 slice. The times are simulated.
32 devices in a mesh: groups: 2 (over y), latent: 4 (over z), rows: 4 (over x, core).
Axes of the slice: x: 2, y: 2, z: 4, core: 2. Of those that a mesh axis runs over, the one named last changes fastest.
Arguments:
- activations_in: bfloat16 [2, 128, 2304], P('groups', None, 'latent'), parts along dimension 0, may hold values from -6 to 6
- gate_proj: bfloat16 [2304, 4608], P('rows', 'latent'), may hold values from -0.125 to 0.125
- up_proj: bfloat16 [2304, 4608], P('rows', 'latent'), may hold values from -0.125 to 0.125
- down_proj: bfloat16 [4608, 2304], P('latent', 'rows'), may hold values from -0.09375 to 0.09375
- enc_weight: bfloat16 [4608, 65536], P(('groups', 'rows'), 'latent'), parts along dimension 0, may hold values from -6 to 6
- enc_bias: float32 [131072], P(('groups', 'latent')), parts along dimension 0, may hold values from -0.5 to 0.5
- dec_weight: bfloat16 [131072, 2304], P(('groups', 'latent'), 'rows'), parts along dimension 0, may hold values from -6 to 6
- dec_bias: float32 [4608], P(('groups', 'rows')), parts along dimension 0, may hold values from -0.5 to 0.5
Outputs:
- enc_weight_new: bfloat16 [4608, 65536], P(('groups', 'rows'), 'latent'), parts along dimension 0
- enc_bias_new: float32 [131072], P(('groups', 'latent')), parts along dimension 0
- dec_weight_new: bfloat16 [131072, 2304], P(('groups', 'latent'), 'rows'), parts along dimension 0
- dec_bias_new: float32 [4608], P(('groups', 'rows')), parts along dimension 0
There are 2 independent parts, one for each index of `groups`. A program takes and returns all parts, laid end to end along the dimension named above; an argument that names none is the same for every part. Nothing has to cross between parts.
All inputs are finite; a program needn't handle non-finite values.
Results may differ from a plain program's by a relative error of at most 0.02.
Values may be sent and summed in bfloat16 or wider, within the bound.
A program may use at most 128 MiB of HBM per device.

v0:
```python
import functools

import jax
import jax.numpy as jnp
from jax import lax
from jax.experimental import pallas as pl
from jax.experimental.pallas import tpu as pltpu
from jax.sharding import PartitionSpec as P

MODEL_WIDTH = 2304
LATENTS = 65536


sparsity_cost = 0.1
sharpness = 8.0
weight_rate = 2.0
enc_bias_rate = 0.01
dec_bias_rate = 0.002

BF16 = jnp.bfloat16
F32 = jnp.float32
CHUNKS = 8


def swap(x, axis, n, bit):
    return lax.ppermute(x, axis, [(i, i ^ bit) for i in range(n)])


def halves_scatter(x, axis, n, wire):
    me = lax.axis_index(axis)
    bit = 1
    while bit < n:
        size = x.shape[0] // 2
        mine = (me // bit) % 2
        keep = lax.dynamic_slice_in_dim(x, mine * size, size, 0)
        give = lax.dynamic_slice_in_dim(x, (1 - mine) * size, size, 0)
        got = swap(give.astype(wire), axis, n, bit)
        x = keep.astype(F32) + got.astype(F32)
        bit *= 2
    return x


def halves_gather(x, axis, n):
    me = lax.axis_index(axis)
    bit = n // 2
    while bit >= 1:
        got = swap(x, axis, n, bit)
        first = ((me // bit) % 2) == 0
        x = jnp.concatenate([jnp.where(first, x, got), jnp.where(first, got, x)], axis=0)
        bit //= 2
    return x


def direct_scatter(x, axis, n, wire):
    me = lax.axis_index(axis)
    size = x.shape[0] // n
    total = lax.dynamic_slice_in_dim(x, me * size, size, 0)
    gots = []
    for shift in range(1, n):
        to = lax.rem(me + shift, n)
        give = lax.dynamic_slice_in_dim(x, to * size, size, 0).astype(wire)
        gots.append(lax.ppermute(give, axis, [(i, (i + shift) % n) for i in range(n)]))
    for got in gots:
        total = total + got.astype(F32)
    return total


def direct_gather(x, axis, n):
    me = lax.axis_index(axis)
    size = x.shape[0]
    out = jnp.zeros((size * n,) + x.shape[1:], x.dtype)
    parts = [(me, x)]
    for shift in range(1, n):
        got = lax.ppermute(x, axis, [(i, (i + shift) % n) for i in range(n)])
        parts.append((lax.rem(me - shift + n, n), got))
    for at, part in parts:
        out = lax.dynamic_update_slice_in_dim(out, part, at * size, 0)
    return out


def update_kernel(rate, has_buf, left_ref, right_ref, w_ref, *rest):
    out_ref, sums_ref = rest[1:] if has_buf else rest
    right = right_ref[...]
    grad = jnp.dot(left_ref[...], right, preferred_element_type=F32)
    out_ref[...] = (w_ref[...].astype(F32) - rate * grad).astype(out_ref.dtype)
    ones = jnp.ones((8, right.shape[0]), right.dtype)
    sums_ref[...] = jnp.dot(ones, right, preferred_element_type=F32)


def update(rate, left, right, weight, first, buf, grant):
    depth, tokens = left.shape
    columns = right.shape[1]
    tile = min(2048, columns)
    base = first // tile
    block = pl.BlockSpec((depth, tile), lambda i: (0, base + i))
    in_specs = [
        pl.BlockSpec((depth, tokens), lambda i: (0, 0)),
        pl.BlockSpec((tokens, tile), lambda i: (0, i)),
        block,
    ]
    args = [left, right, weight]
    if buf is not None:
        in_specs.append(pl.BlockSpec(memory_space=pl.ANY))
        args.append(buf)
    return pl.pallas_call(
        functools.partial(update_kernel, rate, buf is not None),
        grid=(columns // tile,),
        out_shape=(
            jax.ShapeDtypeStruct(weight.shape, weight.dtype),
            jax.ShapeDtypeStruct((8, columns), F32),
        ),
        in_specs=in_specs,
        out_specs=(block, pl.BlockSpec((8, tile), lambda i: (0, i))),
        input_output_aliases={} if buf is None else {3: 0},
        compiler_params=pltpu.CompilerParams(vmem_limit_bytes=grant),
        cost_estimate=pl.CostEstimate(
            flops=2 * depth * tokens * columns, bytes_accessed=4 * depth * columns, transcendentals=0
        ),
    )(*args)


def body(n_latent, n_rows, activations_in, gate_proj, up_proj, down_proj, enc_weight, enc_bias, dec_weight, dec_bias):
    tokens = activations_in.shape[1]
    width, local = enc_weight.shape
    here = activations_in.reshape(tokens, activations_in.shape[2])
    if n_latent == n_rows:
        pairs = [(a * n_rows + b, b * n_rows + a) for a in range(n_latent) for b in range(n_rows)]
        portion = lax.ppermute(here, ("latent", "rows"), pairs)
    else:
        everything = lax.all_gather(here, "latent", axis=1, tiled=True)
        portion = lax.dynamic_slice_in_dim(everything, lax.axis_index("rows") * width, width, 1)
    if n_latent <= 8:
        scatter_l = lambda v, wire: direct_scatter(v, "latent", n_latent, wire)
        gather_l = lambda v: direct_gather(v, "latent", n_latent)
    else:
        scatter_l = lambda v, wire: lax.psum_scatter(v, "latent", scatter_dimension=0, tiled=True)
        gather_l = lambda v: lax.all_gather(v, "latent", axis=0, tiled=True)

    gate_part = jnp.dot(portion, gate_proj, preferred_element_type=F32)
    up_part = jnp.dot(portion, up_proj, preferred_element_type=F32)
    both = jnp.concatenate([gate_part, up_part], axis=1).astype(BF16)
    both = halves_scatter(both, "rows", n_rows, BF16)
    gate_term, up_term = both[:, :gate_proj.shape[1]], both[:, gate_proj.shape[1]:]
    hidden = (jax.nn.gelu(gate_term, approximate=True) * up_term).astype(BF16)
    hidden = halves_gather(hidden, "rows", n_rows)
    partial_value = lax.dot_general(down_proj, hidden, (((0,), (1,)), ((), ())), preferred_element_type=F32)
    inputs_here = scatter_l(partial_value, BF16).astype(BF16)
    inputs = gather_l(inputs_here)
    share = inputs_here.shape[0]
    bias_here = lax.dynamic_slice_in_dim(dec_bias, lax.axis_index("latent") * share, share, 0)

    enc_scale = MODEL_WIDTH ** (-0.5)
    dec_scale = LATENTS ** (-0.5)
    dec_turned = dec_weight.T
    chunks = max(1, min(4, local // 512))
    step = local // chunks
    spans = [slice(c * step, (c + 1) * step) for c in range(chunks)]
    over_width = (((0,), (0,)), ((), ()))
    local_rebuilt = jnp.zeros((width, tokens), F32)
    latents, pres = [], []
    for span in spans:
        part = lax.dot_general(inputs, enc_weight[:, span], over_width, preferred_element_type=F32).astype(BF16)
        encoded = halves_scatter(part, "rows", n_rows, BF16)
        pre = enc_scale * encoded + enc_bias[span]
        pres.append(pre)
        mine = (jax.nn.softplus(sharpness * pre) / sharpness).astype(BF16)
        full = halves_gather(mine, "rows", n_rows)
        latents.append(full)
        local_rebuilt = local_rebuilt + lax.dot_general(
            dec_turned[:, span], full, (((1,), (1,)), ((), ())), preferred_element_type=F32
        )
    rebuilt_share = scatter_l(local_rebuilt, F32)
    grad_share = (
        2.0 * (dec_scale * rebuilt_share + bias_here[:, None] - inputs_here.astype(F32))
    ).astype(BF16)
    residual_grad = gather_l(grad_share)
    grads = []
    for c, span in enumerate(spans):
        part = lax.dot_general(residual_grad, dec_turned[:, span], over_width, preferred_element_type=F32).astype(BF16)
        back = halves_scatter(part, "rows", n_rows, BF16)
        mine = (jax.nn.sigmoid(sharpness * pres[c]) * (dec_scale * back + sparsity_cost)).astype(BF16)
        grads.append(halves_gather(mine, "rows", n_rows))
    dec_new = enc_new = None
    for c, span in enumerate(spans):
        dec_new, _ = update(weight_rate * dec_scale, residual_grad, latents[c], dec_turned, c * step, dec_new, 24 << 20)
    sums = []
    for c, span in enumerate(spans):
        enc_new, total = update(weight_rate * enc_scale, inputs, grads[c], enc_weight, c * step, enc_new, 52 << 20)
        sums.append(total[0])
    enc_bias = enc_bias - enc_bias_rate * jnp.concatenate(sums)
    dec_bias = dec_bias - dec_bias_rate * jnp.sum(residual_grad, axis=1, dtype=F32)
    return (enc_new, enc_bias, dec_new.T, dec_bias)


MESH = pl.DeviceIdType.MESH
HALVES = 2
LEAD = 3
RING = 4


def softplus(v):
    return jnp.maximum(v, 0.0) + jnp.log1p(jnp.exp(-jnp.abs(v)))


def over_last(a, b):
    return lax.dot_general(a, b, (((1,), (1,)), ((), ())), preferred_element_type=F32)


def train_kernel(
    n_latent, n_rows, chunk,
    act_ref, gate_ref, up_ref, down_ref, enc_ref, bias_ref, dec_ref, dec_bias_ref,
    lat_out, grad_out, x_out, resid_out,
    act_turned, act_own, act, gate_up, down, enc, dec,
    ffn_part, ffn_got, ffn_sum, ffn_far, hidden,
    acc, value, value_got, share, features, resid_got, resid_share, resid,
    part, got, pair, far_got, latents, grads,
    load_sem, weight_sem, act_send, act_sem, ffn_send, ffn_sem, z_send, z_sem,
    part_send, part_sem, pair_send, pair_sem, full_send, full_sem, out_sem,
):
    rows = lax.axis_index("rows")
    z = lax.axis_index("latent")
    core = lax.rem(rows, 2)
    mate = {"rows": rows + 1 - 2 * core}
    far = {"rows": lax.rem(rows + 2, n_rows)}
    others = [{"latent": lax.rem(z + s, n_latent)} for s in range(1, n_latent)]
    half = act.shape[1]
    own = half // 2
    small = half // n_latent
    _, local_hidden = gate_ref.shape
    count = enc.shape[0]
    items = HALVES * count
    mine = pl.ds(pl.multiple_of(core * own, own), own)
    theirs = pl.ds(pl.multiple_of((1 - core) * own, own), own)
    small_of = lambda at: pl.ds(pl.multiple_of(at * small, small), small)
    my_small = small_of(z)

    def remote(src, dst, send, recv, to):
        return pltpu.make_async_remote_copy(
            src_ref=src, dst_ref=dst, send_sem=send, recv_sem=recv, device_id=to, device_id_type=MESH
        )

    loads = [
        pltpu.make_async_copy(act_ref, act_turned, load_sem.at[0]),
        pltpu.make_async_copy(gate_ref, gate_up.at[:, :local_hidden], load_sem.at[1]),
        pltpu.make_async_copy(up_ref, gate_up.at[:, local_hidden:], load_sem.at[2]),
        pltpu.make_async_copy(down_ref, down, load_sem.at[3]),
    ]
    for load in loads:
        load.start()
    weights = []
    for c in range(count):
        span = slice(c * chunk, (c + 1) * chunk)
        weights.append(pltpu.make_async_copy(enc_ref.at[:, span], enc.at[c], weight_sem.at[0, c]))
        weights.append(pltpu.make_async_copy(dec_ref.at[:, span], dec.at[c], weight_sem.at[1, c]))
    for load in weights:
        load.start()

    barrier = pltpu.get_barrier_semaphore()
    for to in [mate, far] + others:
        pl.semaphore_signal(barrier, inc=1, device_id=to, device_id_type=MESH)
    loads[0].wait()
    turned = act_turned[...].T
    for h in range(HALVES):
        act_own[h] = turned[h * half:(h + 1) * half]
    pl.semaphore_wait(barrier, n_latent + 1)

    def act_copy(h, s):
        return remote(act_own.at[h], act.at[h], act_send.at[h, s], act_sem.at[h], others[s])

    @pl.when(z == rows)
    def _():
        for h in range(HALVES):
            for s in reversed(range(n_latent - 1)):
                act_copy(h, s).start()
        for h in range(HALVES):
            act[h] = act_own[h]

    @pl.when(z != rows)
    def _():
        act_copy(0, 0).wait_recv()

    loads[1].wait()
    loads[2].wait()

    def ffn_copy(stage, h):
        src, dst, to = (
            (ffn_part.at[h, theirs], ffn_got.at[h], mate),
            (ffn_sum.at[h], ffn_far.at[h], far),
            (hidden.at[h, mine], hidden.at[h, mine], mate),
        )[stage]
        return remote(src, dst, ffn_send.at[stage, h], ffn_sem.at[stage, h], to)

    def z_copies(stage, h):
        copies = []
        for s in range(n_latent - 1):
            to = lax.rem(z + s + 1, n_latent)
            src, dst = (
                (value.at[h, small_of(to)], value_got.at[h, s]),
                (share.at[h], features.at[h, my_small]),
                (acc.at[h, small_of(to)], resid_got.at[h, s]),
                (resid_share.at[h], resid.at[h, my_small]),
            )[stage]
            copies.append(remote(src, dst, z_send.at[stage, h, s], z_sem.at[stage, h, s], others[s]))
        return copies

    for h in range(HALVES):
        if h > 0:
            @pl.when(z != rows)
            def _():
                act_copy(h, 0).wait_recv()
        ffn_part[h] = jnp.dot(act[h], gate_up[...], preferred_element_type=F32).astype(BF16)
        ffn_copy(0, h).start()
    for h in range(HALVES):
        ffn_copy(0, h).wait_recv()
        ffn_sum[h] = (ffn_part[h, mine].astype(F32) + ffn_got[h].astype(F32)).astype(BF16)
        ffn_copy(1, h).start()
    for h in range(HALVES):
        ffn_copy(1, h).wait_recv()
        total = ffn_sum[h].astype(F32) + ffn_far[h].astype(F32)
        gate_term, up_term = total[:, :local_hidden], total[:, local_hidden:]
        hidden[h, mine] = (jax.nn.gelu(gate_term, approximate=True) * up_term).astype(BF16)
        ffn_copy(2, h).start()
    loads[3].wait()
    for h in range(HALVES):
        ffn_copy(2, h).wait_recv()
        part_value = over_last(hidden[h], down[...])
        acc[h] = part_value
        value[h] = part_value.astype(BF16)
        for copy in z_copies(0, h):
            copy.start()
    for h in range(HALVES):
        total = acc[h, my_small]
        for s, copy in enumerate(z_copies(0, h)):
            copy.wait_recv()
            total = total + value_got[h, s].astype(F32)
        share[h] = total.astype(BF16)
        features[h, my_small] = total.astype(BF16)
        for copy in z_copies(1, h):
            copy.start()
        acc[h] = jnp.zeros_like(acc[h])
    for load in weights:
        load.wait()
    for copy in z_copies(1, 0):
        copy.wait_recv()

    enc_scale = MODEL_WIDTH ** (-0.5)
    dec_scale = LATENTS ** (-0.5)

    def near_copy(i):
        slot = lax.rem(i, RING)
        return remote(part.at[slot, theirs], got.at[lax.rem(i, items)], part_send.at[slot], part_sem.at[i], mate)

    def far_copy(i):
        return remote(pair.at[i], far_got.at[i], pair_send.at[i], pair_sem.at[i], far)

    def full_copy(i, full, j):
        return remote(full.at[j, mine], full.at[j, mine], full_send.at[i], full_sem.at[i], mate)

    def out_copy(i, full, j, out):
        h, c = j // count, lax.rem(j, count)
        dst = out.at[
            pl.ds(pl.multiple_of(h * half, half), half), pl.ds(pl.multiple_of(c * chunk, chunk), chunk)
        ]
        return pltpu.make_async_copy(full.at[j], dst, out_sem.at[i])

    def dot_step(i, phase, reuse):
        j = i - phase * items
        h, c = j // count, lax.rem(j, count)
        if reuse:
            near_copy(i - RING).wait_send()
        left, right = ((features, enc), (resid, dec))[phase]
        slot = lax.rem(i, RING)
        part[slot] = jnp.dot(left[h], right[c], preferred_element_type=F32).astype(BF16)
        near_copy(i).start()

    def pair_step(i):
        near_copy(i).wait_recv()
        slot = lax.rem(i, RING)
        pair[i] = (part[slot, mine].astype(F32) + got[lax.rem(i, items)].astype(F32)).astype(BF16)
        far_copy(i).start()

    def pre_of(j):
        return enc_scale * (pair[j].astype(F32) + far_got[j].astype(F32)) + bias_ref[lax.rem(j, count)]

    def full_step(i, phase):
        j = i - phase * items
        far_copy(i).wait_recv()
        if phase == 0:
            latents[j, mine] = (softplus(sharpness * pre_of(j)) / sharpness).astype(BF16)
            full_copy(i, latents, j).start()
        else:
            back = pair[i].astype(F32) + far_got[i].astype(F32)
            slope = jax.nn.sigmoid(sharpness * pre_of(j))
            grads[j, mine] = (slope * (dec_scale * back + sparsity_cost)).astype(BF16)
            full_copy(i, grads, j).start()

    def use_step(i, phase):
        j = i - phase * items
        full, out = ((latents, lat_out), (grads, grad_out))[phase]
        full_copy(i, full, j).wait_recv()
        if phase == 0:
            h, c = j // count, lax.rem(j, count)
            acc[h] += over_last(full[j], dec[c])
        out_copy(i, full, j, out).start()

    def run(first, last):
        if last <= first:
            return

        def body(i, carry):
            if first + LEAD < 2 * items:
                dot_step(i + LEAD, (first + LEAD) // items, True)
            if first + LEAD - 1 < 2 * items:
                pair_step(i + LEAD - 1)
            full_step(i, first // items)
            use_step(i - 1, (first - 1) // items)
            return carry

        lax.fori_loop(first, last, body, 0)

    def resid_step(h):
        total = acc[h, my_small]
        for s, copy in enumerate(z_copies(2, h)):
            copy.wait_recv()
            total = total + resid_got[h, s]
        grad = 2.0 * (dec_scale * total + dec_bias_ref[...] - share[h].astype(F32))
        resid_share[h] = grad.astype(BF16)
        resid[h, my_small] = grad.astype(BF16)
        for copy in z_copies(3, h):
            copy.start()

    for i in range(LEAD):
        dot_step(i, 0, False)
    for i in range(LEAD - 1):
        pair_step(i)
    dot_step(LEAD, 0, LEAD >= RING)
    pair_step(LEAD - 1)
    full_step(0, 0)
    marks = {}
    for h in range(HALVES):
        marks.setdefault((h + 1) * count + 1, []).append(lambda h=h: [copy.start() for copy in z_copies(2, h)])
        marks.setdefault((h + 1) * count + 3, []).append(lambda h=h: resid_step(h))
        marks.setdefault(items + h * count - LEAD, []).append(
            lambda h=h: [copy.wait_recv() for copy in z_copies(3, h)]
        )
        if h > 0:
            marks.setdefault(h * count - LEAD, []).append(lambda h=h: [copy.wait_recv() for copy in z_copies(1, h)])
    cuts = set(marks) | {1, items - LEAD, items - LEAD + 1, items, items + 1}
    cuts |= {2 * items - LEAD, 2 * items - LEAD + 1, 2 * items}
    cuts = sorted(cuts)
    for first, last in zip(cuts[:-1], cuts[1:]):
        for act_on in marks.get(first, []):
            act_on()
        run(first, last)
    use_step(2 * items - 1, 1)

    for h in range(HALVES):
        x_out[h * half:(h + 1) * half] = features[h]
        resid_out[h * half:(h + 1) * half] = resid[h]

    @pl.when(z == rows)
    def _():
        for h in range(HALVES):
            for s in range(n_latent - 1):
                act_copy(h, s).wait_send()

    for h in range(HALVES):
        for stage in range(3):
            ffn_copy(stage, h).wait_send()
        for stage in range(4):
            for copy in z_copies(stage, h):
                copy.wait_send()
    for i in range(2 * items - RING, 2 * items):
        near_copy(i).wait_send()

    def drain(i, carry):
        for phase, full, out in ((0, latents, lat_out), (1, grads, grad_out)):
            at = i + phase * items
            far_copy(at).wait_send()
            full_copy(at, full, i).wait_send()
            out_copy(at, full, i, out).wait()
        return carry

    lax.fori_loop(0, items, drain, 0)


def fast_body(n_latent, n_rows, activations_in, gate_proj, up_proj, down_proj, enc_weight, enc_bias, dec_weight, dec_bias):
    tokens = activations_in.shape[1]
    width, local = enc_weight.shape
    hidden = gate_proj.shape[1]
    chunk = local // CHUNKS
    half = tokens // HALVES
    own, small, items = half // 2, half // n_latent, HALVES * CHUNKS
    dec_turned = dec_weight.T
    any_spec = pl.BlockSpec(memory_space=pl.ANY)
    vmem_spec = pl.BlockSpec(memory_space=pltpu.VMEM)
    vmem, dma = pltpu.VMEM, pltpu.SemaphoreType.DMA
    between = n_latent - 1
    latents, grads, inputs, residual_grad = pl.pallas_call(
        functools.partial(train_kernel, n_latent, n_rows, chunk),
        out_shape=(
            jax.ShapeDtypeStruct((tokens, local), BF16),
            jax.ShapeDtypeStruct((tokens, local), BF16),
            jax.ShapeDtypeStruct((tokens, width), BF16),
            jax.ShapeDtypeStruct((tokens, width), BF16),
        ),
        in_specs=[any_spec] * 5 + [vmem_spec, any_spec, vmem_spec],
        out_specs=(any_spec, any_spec, vmem_spec, vmem_spec),
        scratch_shapes=[
            vmem((width, tokens), BF16),
            vmem((HALVES, half, width), BF16),
            vmem((HALVES, half, width), BF16),
            vmem((width, 2 * hidden), BF16),
            vmem((width, hidden), BF16),
            vmem((CHUNKS, width, chunk), BF16),
            vmem((CHUNKS, width, chunk), BF16),
            vmem((HALVES, half, 2 * hidden), BF16),
            vmem((HALVES, own, 2 * hidden), BF16),
            vmem((HALVES, own, 2 * hidden), BF16),
            vmem((HALVES, own, 2 * hidden), BF16),
            vmem((HALVES, half, hidden), BF16),
            vmem((HALVES, half, width), F32),
            vmem((HALVES, half, width), BF16),
            vmem((HALVES, between, small, width), BF16),
            vmem((HALVES, small, width), BF16),
            vmem((HALVES, half, width), BF16),
            vmem((HALVES, between, small, width), F32),
            vmem((HALVES, small, width), BF16),
            vmem((HALVES, half, width), BF16),
            vmem((RING, half, chunk), BF16),
            vmem((items, own, chunk), BF16),
            vmem((2 * items, own, chunk), BF16),
            vmem((2 * items, own, chunk), BF16),
            vmem((items, half, chunk), BF16),
            vmem((items, half, chunk), BF16),
            dma((4,)),
            dma((2, CHUNKS)),
            dma((HALVES, between)),
            dma((HALVES,)),
            dma((3, HALVES)),
            dma((3, HALVES)),
            dma((4, HALVES, between)),
            dma((4, HALVES, between)),
            dma((RING,)),
            dma((2 * items,)),
            dma((2 * items,)),
            dma((2 * items,)),
            dma((2 * items,)),
            dma((2 * items,)),
            dma((2 * items,)),
        ],
        compiler_params=pltpu.CompilerParams(collective_id=0, has_side_effects=True, vmem_limit_bytes=67043328),
    )(
        activations_in.reshape(tokens, activations_in.shape[2]).T, gate_proj, up_proj, down_proj.T, enc_weight,
        enc_bias.reshape(CHUNKS, 1, chunk), dec_turned, dec_bias.reshape(1, width),
    )
    enc_scale = MODEL_WIDTH ** (-0.5)
    dec_scale = LATENTS ** (-0.5)
    dec_new, _ = update(weight_rate * dec_scale, residual_grad.T, latents, dec_turned, 0, None, 24 << 20)
    enc_new, total = update(weight_rate * enc_scale, inputs.T, grads, enc_weight, 0, None, 24 << 20)
    enc_bias = enc_bias - enc_bias_rate * total[0]
    dec_bias = dec_bias - dec_bias_rate * jnp.sum(residual_grad, axis=0, dtype=F32)
    return (enc_new, enc_bias, dec_new.T, dec_bias)


def solution(mesh):
    def step(*args):
        return run(mesh.shape["latent"], mesh.shape["rows"], *args)

    small = mesh.shape["latent"] == mesh.shape["rows"] == 4
    run = fast_body if small else body


    return jax.shard_map(
        step,
        mesh=mesh,
        in_specs=(
            P("groups", None, "latent"),
            P("rows", "latent"),
            P("rows", "latent"),
            P("latent", "rows"),
            P(("groups", "rows"), "latent"),
            P(("groups", "latent")),
            P(("groups", "latent"), "rows"),
            P(("groups", "rows")),
        ),
        out_specs=(
            P(("groups", "rows"), "latent"),
            P(("groups", "latent")),
            P(("groups", "latent"), "rows"),
            P(("groups", "rows")),
        ),
        check_vma=False,
    )
```

profile of v0, /device:TPU:3, one launch (start us, length us, event | category | flops | bytes accessed | tf_op | source)
XLA Modules:
  0.0 180.0 jit_solution(14660902081997663930)
XLA Ops:
  0.6 1.3 reshape.21.dec_bias_ref
  1.9 137.1 %shard_map.111 = (bf16[128,16384]{1,0:T(8,128)(2,1)}, bf16[128,16384]{1,0:T(8,128)(2,1)}, bf16[128,576]{1,0:T(8,128)(2,1)}, bf16[128,576]{1,0:T(8,128)(2,1)}) custom-call(bf16[576,128]{1,0:T(8,128)(2,1)} %bitcast.17, bf16[576,1152]{1,0:T(8,128)(2,1)} %gate_ref.1, bf16[576,1152]{1,0:T(8,128)(2,1)} %up_ref.1, bf16[576,1152]{1,0:T(8,128)(2,1)} %bitcast.14, ...), custom_call_target="tpu_custom_call" | custom-call | tf_op jit(solution)/shard_map/pallas_call | solution.py:499
  139.0 1.1 copy.12
  140.1 1.0 convert_reduce_fusion
  141.1 1.1 copy.13
  142.1 1.3 multiply_subtract_fusion
  143.4 0.0 copy-start
  143.4 6.4 %copy-done = bf16[576,16384]{1,0:T(8,128)(2,1)S(1)} copy-done((bf16[576,16384]{1,0:T(8,128)(2,1)S(1)}, bf16[576,16384]{1,0:T(8,128)(2,1)}, u32[]{:S(2)}) %copy-start) | copy-done | bytes 18874392
  149.8 0.0 copy-start.3
  149.8 2.2 %copy-done.3 = bf16[128,16384]{1,0:T(8,128)(2,1)S(1)} copy-done((bf16[128,16384]{1,0:T(8,128)(2,1)S(1)}, bf16[128,16384]{1,0:T(8,128)(2,1)}, u32[]{:S(2)}) %copy-start.3) | copy-done | bytes 4194328
  152.0 0.0 copy-start.4
  152.0 0.0 copy-start.2
  152.0 10.5 %shard_map.112 = (bf16[576,16384]{1,0:T(8,128)(2,1)}, f32[8,16384]{1,0:T(8,128)S(1)}) custom-call(bf16[576,128]{1,0:T(8,128)(2,1)S(1)} %bitcast.13, bf16[128,16384]{1,0:T(8,128)(2,1)S(1)} %copy-done.3, bf16[576,16384]{1,0:T(8,128)(2,1)S(1)} %copy-done), custom_call_target="tpu_custom_call" | custom-call | flops 2415919104 | bytes 37748736 | tf_op jit(solution)/shard_map/pallas_call | solution.py:105
  162.4 0.1 slice_multiply_fusion
  162.5 0.0 copy-done.4
  162.5 0.6 sub.6
  163.1 0.0 copy-done.2
  163.1 0.0 copy-start.1
  163.1 6.4 %copy-done.1 = bf16[16384,576]{0,1:T(8,128)(2,1)S(1)} copy-done((bf16[16384,576]{0,1:T(8,128)(2,1)S(1)}, bf16[16384,576]{0,1:T(8,128)(2,1)}, u32[]{:S(2)}) %copy-start.1) | copy-done | bytes 18874392
  169.5 10.5 %shard_map.113 = (bf16[576,16384]{1,0:T(8,128)(2,1)}, f32[8,16384]{1,0:T(8,128)}) custom-call(bf16[576,128]{1,0:T(8,128)(2,1)S(1)} %bitcast.12, bf16[128,16384]{1,0:T(8,128)(2,1)S(1)} %copy-done.2, bf16[576,16384]{1,0:T(8,128)(2,1)S(1)} %bitcast.11), custom_call_target="tpu_custom_call" | custom-call | flops 2415919104 | bytes 37748736 | tf_op jit(solution)/shard_map/pallas_call | solution.py:105
Async XLA Ops:
  143.4 6.4 %copy-start = (bf16[576,16384]{1,0:T(8,128)(2,1)S(1)}, bf16[576,16384]{1,0:T(8,128)(2,1)}, u32[]{:S(2)}) copy-start(bf16[576,16384]{1,0:T(8,128)(2,1)} %w_ref.1) | copy-start | bytes 56623108
  149.8 2.2 %copy-start.3 = (bf16[128,16384]{1,0:T(8,128)(2,1)S(1)}, bf16[128,16384]{1,0:T(8,128)(2,1)}, u32[]{:S(2)}) copy-start(bf16[128,16384]{1,0:T(8,128)(2,1)} %get-tuple-element.12.right_ref) | copy-start | bytes 12582916
  152.0 10.5 %copy-start.4 = (f32[16384]{0:T(1024)S(1)}, f32[16384]{0:T(1024)}, u32[]{:S(2)}) copy-start(f32[16384]{0:T(1024)} %param.13) | copy-start | bytes 196612
  152.0 11.2 %copy-start.2 = (bf16[128,16384]{1,0:T(8,128)(2,1)S(1)}, bf16[128,16384]{1,0:T(8,128)(2,1)}, u32[]{:S(2)}) copy-start(bf16[128,16384]{1,0:T(8,128)(2,1)} %get-tuple-element.16.right_ref) | copy-start | bytes 12582916
  163.1 6.4 %copy-start.1 = (bf16[16384,576]{0,1:T(8,128)(2,1)S(1)}, bf16[16384,576]{0,1:T(8,128)(2,1)}, u32[]{:S(2)}) copy-start(bf16[16384,576]{0,1:T(8,128)(2,1)} %param.14) | copy-start | bytes 56623108
where the time goes:
time: 180 us
  Pallas kernels  158 us (88%)
  local copies, waits for them, and re-layouts  18.3 us (10%)
  other arithmetic  2.95 us (2%)
    pallas_call x1, Pallas kernels, fast_body(): pl.pallas_call(functools.partial(train_kernel, n_latent, n_rows, chunk),...  137 us
    pallas_call x2, Pallas kernels, update(): pl.pallas_call(functools.partial(update_kernel, rate, buf is not None), g...  20.9 us
    unnamed x10, local copies, waits for them, and re-layouts  14.9 us

commit v1 on v0

--- a/solution.py
+++ b/solution.py
@@ -20,6 +20,8 @@
 BF16 = jnp.bfloat16
 F32 = jnp.float32
 CHUNKS = 8
+TILE = 256
+GRANT = 23 << 20
 
 
 def swap(x, axis, n, bit):
@@ -209,13 +211,13 @@
 def train_kernel(
     n_latent, n_rows, chunk,
     act_ref, gate_ref, up_ref, down_ref, enc_ref, bias_ref, dec_ref, dec_bias_ref,
-    lat_out, grad_out, x_out, resid_out,
-    act_turned, act_own, act, gate_up, down, enc, dec,
+    enc, dec, grads, features, resid,
+    act_turned, act_own, act, gate_up, down,
     ffn_part, ffn_got, ffn_sum, ffn_far, hidden,
-    acc, value, value_got, share, features, resid_got, resid_share, resid,
-    part, got, pair, far_got, latents, grads,
+    acc, value, value_got, share, resid_got, resid_share, resid_turned,
+    part, pair, far_got, latents,
     load_sem, weight_sem, act_send, act_sem, ffn_send, ffn_sem, z_send, z_sem,
-    part_send, part_sem, pair_send, pair_sem, full_send, full_sem, out_sem,
+    part_send, part_sem, pair_send, pair_sem, full_send, full_sem,
 ):
     rows = lax.axis_index("rows")
     z = lax.axis_index("latent")
@@ -348,20 +350,13 @@
 
     def near_copy(i):
         slot = lax.rem(i, RING)
-        return remote(part.at[slot, theirs], got.at[lax.rem(i, items)], part_send.at[slot], part_sem.at[i], mate)
+        return remote(part.at[slot, theirs], grads.at[lax.rem(i, items), theirs], part_send.at[slot], part_sem.at[i], mate)
 
     def far_copy(i):
         return remote(pair.at[i], far_got.at[i], pair_send.at[i], pair_sem.at[i], far)
 
     def full_copy(i, full, j):
         return remote(full.at[j, mine], full.at[j, mine], full_send.at[i], full_sem.at[i], mate)
-
-    def out_copy(i, full, j, out):
-        h, c = j // count, lax.rem(j, count)
-        dst = out.at[
-            pl.ds(pl.multiple_of(h * half, half), half), pl.ds(pl.multiple_of(c * chunk, chunk), chunk)
-        ]
-        return pltpu.make_async_copy(full.at[j], dst, out_sem.at[i])
 
     def dot_step(i, phase, reuse):
         j = i - phase * items
@@ -376,7 +371,7 @@
     def pair_step(i):
         near_copy(i).wait_recv()
         slot = lax.rem(i, RING)
-        pair[i] = (part[slot, mine].astype(F32) + got[lax.rem(i, items)].astype(F32)).astype(BF16)
+        pair[i] = (part[slot, mine].astype(F32) + grads[lax.rem(i, items), mine].astype(F32)).astype(BF16)
         far_copy(i).start()
 
     def pre_of(j):
@@ -396,12 +391,26 @@
 
     def use_step(i, phase):
         j = i - phase * items
-        full, out = ((latents, lat_out), (grads, grad_out))[phase]
+        full = (latents, grads)[phase]
         full_copy(i, full, j).wait_recv()
         if phase == 0:
             h, c = j // count, lax.rem(j, count)
             acc[h] += over_last(full[j], dec[c])
-        out_copy(i, full, j, out).start()
+
+    def turn_resid():
+        resid_turned[...] = jnp.concatenate([resid[h] for h in range(HALVES)], axis=0).T
+
+    def dec_step(c):
+        def tile_step(t, carry):
+            span = pl.ds(pl.multiple_of(t * TILE, TILE), TILE)
+            right = jnp.concatenate([latents[h * count + c, :, span] for h in range(HALVES)], axis=0)
+            grad = jnp.dot(resid_turned[...], right, preferred_element_type=F32)
+            dec[c, :, span] = (dec[c, :, span].astype(F32) - weight_rate * dec_scale * grad).astype(BF16)
+            return carry
+
+        lax.fori_loop(0, chunk // TILE, tile_step, 0)
+
+    last_dots = 2 * items - count - LEAD + 1
 
     def run(first, last):
         if last <= first:
@@ -414,6 +423,8 @@
                 pair_step(i + LEAD - 1)
             full_step(i, first // items)
             use_step(i - 1, (first - 1) // items)
+            if last_dots <= first < last_dots + count:
+                dec_step(i - last_dots)
             return carry
 
         lax.fori_loop(first, last, body, 0)
@@ -445,18 +456,15 @@
         )
         if h > 0:
             marks.setdefault(h * count - LEAD, []).append(lambda h=h: [copy.wait_recv() for copy in z_copies(1, h)])
+    marks.setdefault(last_dots, []).append(turn_resid)
     cuts = set(marks) | {1, items - LEAD, items - LEAD + 1, items, items + 1}
-    cuts |= {2 * items - LEAD, 2 * items - LEAD + 1, 2 * items}
+    cuts |= {2 * items - LEAD, 2 * items - LEAD + 1, last_dots + count, 2 * items}
     cuts = sorted(cuts)
     for first, last in zip(cuts[:-1], cuts[1:]):
         for act_on in marks.get(first, []):
             act_on()
         run(first, last)
     use_step(2 * items - 1, 1)
-
-    for h in range(HALVES):
-        x_out[h * half:(h + 1) * half] = features[h]
-        resid_out[h * half:(h + 1) * half] = resid[h]
 
     @pl.when(z == rows)
     def _():
@@ -474,14 +482,53 @@
         near_copy(i).wait_send()
 
     def drain(i, carry):
-        for phase, full, out in ((0, latents, lat_out), (1, grads, grad_out)):
+        for phase, full in ((0, latents), (1, grads)):
             at = i + phase * items
             far_copy(at).wait_send()
             full_copy(at, full, i).wait_send()
-            out_copy(at, full, i, out).wait()
         return carry
 
     lax.fori_loop(0, items, drain, 0)
+
+
+def write_kernel(
+    enc, dec, grads, features, resid, bias_ref, dec_bias_ref, enc_out, dec_out, bias_out, dec_bias_out,
+    turned, staged, enc_sem, dec_sem,
+):
+    count, _, chunk = enc.shape
+    enc_rate = weight_rate * MODEL_WIDTH ** (-0.5)
+
+    def out_copies(c):
+        span = slice(c * chunk, (c + 1) * chunk)
+        return (
+            pltpu.make_async_copy(dec.at[c], dec_out.at[:, span], dec_sem.at[c]),
+            pltpu.make_async_copy(staged.at[c % RING], enc_out.at[:, span], enc_sem.at[c]),
+        )
+
+    copies = [out_copies(c) for c in range(count)]
+    turned[...] = jnp.concatenate([features[h] for h in range(HALVES)], axis=0).T
+    for c in range(count):
+        copies[c][0].start()
+        if c >= RING:
+            copies[c - RING][1].wait()
+
+        def tile_step(t, carry):
+            span = pl.ds(pl.multiple_of(t * TILE, TILE), TILE)
+            right = jnp.concatenate([grads[h * count + c, :, span] for h in range(HALVES)], axis=0)
+            grad = jnp.dot(turned[...], right, preferred_element_type=F32)
+            staged[c % RING, :, span] = (enc[c, :, span].astype(F32) - enc_rate * grad).astype(BF16)
+            total = jnp.sum(right.astype(F32), axis=0, keepdims=True)
+            bias_out[c, :, span] = bias_ref[c, :, span] - enc_bias_rate * total
+            return carry
+
+        lax.fori_loop(0, chunk // TILE, tile_step, 0)
+        copies[c][1].start()
+    total = sum(jnp.sum(resid[h].astype(F32), axis=0, keepdims=True) for h in range(HALVES))
+    dec_bias_out[...] = dec_bias_ref[...] - dec_bias_rate * total
+    for c in range(count):
+        copies[c][0].wait()
+        if c >= count - RING:
+            copies[c][1].wait()
 
 
 def fast_body(n_latent, n_rows, activations_in, gate_proj, up_proj, down_proj, enc_weight, enc_bias, dec_weight, dec_bias):
@@ -496,24 +543,23 @@
     vmem_spec = pl.BlockSpec(memory_space=pltpu.VMEM)
     vmem, dma = pltpu.VMEM, pltpu.SemaphoreType.DMA
     between = n_latent - 1
-    latents, grads, inputs, residual_grad = pl.pallas_call(
+    enc_held, dec_held, grads, inputs, residual_grad = pl.pallas_call(
         functools.partial(train_kernel, n_latent, n_rows, chunk),
         out_shape=(
-            jax.ShapeDtypeStruct((tokens, local), BF16),
-            jax.ShapeDtypeStruct((tokens, local), BF16),
-            jax.ShapeDtypeStruct((tokens, width), BF16),
-            jax.ShapeDtypeStruct((tokens, width), BF16),
+            vmem((CHUNKS, width, chunk), BF16),
+            vmem((CHUNKS, width, chunk), BF16),
+            vmem((items, half, chunk), BF16),
+            vmem((HALVES, half, width), BF16),
+            vmem((HALVES, half, width), BF16),
         ),
         in_specs=[any_spec] * 5 + [vmem_spec, any_spec, vmem_spec],
-        out_specs=(any_spec, any_spec, vmem_spec, vmem_spec),
+        out_specs=(vmem_spec,) * 5,
         scratch_shapes=[
             vmem((width, tokens), BF16),
             vmem((HALVES, half, width), BF16),
             vmem((HALVES, half, width), BF16),
             vmem((width, 2 * hidden), BF16),
             vmem((width, hidden), BF16),
-            vmem((CHUNKS, width, chunk), BF16),
-            vmem((CHUNKS, width, chunk), BF16),
             vmem((HALVES, half, 2 * hidden), BF16),
             vmem((HALVES, own, 2 * hidden), BF16),
             vmem((HALVES, own, 2 * hidden), BF16),
@@ -523,15 +569,12 @@
             vmem((HALVES, half, width), BF16),
             vmem((HALVES, between, small, width), BF16),
             vmem((HALVES, small, width), BF16),
-            vmem((HALVES, half, width), BF16),
             vmem((HALVES, between, small, width), F32),
             vmem((HALVES, small, width), BF16),
-            vmem((HALVES, half, width), BF16),
+            vmem((width, tokens), BF16),
             vmem((RING, half, chunk), BF16),
-            vmem((items, own, chunk), BF16),
             vmem((2 * items, own, chunk), BF16),
             vmem((2 * items, own, chunk), BF16),
-            vmem((items, half, chunk), BF16),
             vmem((items, half, chunk), BF16),
             dma((4,)),
             dma((2, CHUNKS)),
@@ -547,20 +590,34 @@
             dma((2 * items,)),
             dma((2 * items,)),
             dma((2 * items,)),
-            dma((2 * items,)),
         ],
-        compiler_params=pltpu.CompilerParams(collective_id=0, has_side_effects=True, vmem_limit_bytes=67043328),
+        compiler_params=pltpu.CompilerParams(collective_id=0, has_side_effects=True, vmem_limit_bytes=GRANT),
     )(
         activations_in.reshape(tokens, activations_in.shape[2]).T, gate_proj, up_proj, down_proj.T, enc_weight,
         enc_bias.reshape(CHUNKS, 1, chunk), dec_turned, dec_bias.reshape(1, width),
     )
-    enc_scale = MODEL_WIDTH ** (-0.5)
-    dec_scale = LATENTS ** (-0.5)
-    dec_new, _ = update(weight_rate * dec_scale, residual_grad.T, latents, dec_turned, 0, None, 24 << 20)
-    enc_new, total = update(weight_rate * enc_scale, inputs.T, grads, enc_weight, 0, None, 24 << 20)
-    enc_bias = enc_bias - enc_bias_rate * total[0]
-    dec_bias = dec_bias - dec_bias_rate * jnp.sum(residual_grad, axis=0, dtype=F32)
-    return (enc_new, enc_bias, dec_new.T, dec_bias)
+    enc_held, dec_held, grads, inputs, residual_grad = (
+        pltpu.with_memory_space_constraint(v, vmem) for v in (enc_held, dec_held, grads, inputs, residual_grad)
+    )
+    enc_new, dec_new, enc_bias, dec_bias = pl.pallas_call(
+        write_kernel,
+        out_shape=(
+            jax.ShapeDtypeStruct((width, local), BF16),
+            jax.ShapeDtypeStruct((width, local), BF16),
+            jax.ShapeDtypeStruct((CHUNKS, 1, chunk), F32),
+            jax.ShapeDtypeStruct((1, width), F32),
+        ),
+        in_specs=[vmem_spec] * 7,
+        out_specs=(any_spec, any_spec, vmem_spec, vmem_spec),
+        scratch_shapes=[
+            vmem((width, tokens), BF16),
+            vmem((RING, width, chunk), BF16),
+            dma((CHUNKS,)),
+            dma((CHUNKS,)),
+        ],
+        compiler_params=pltpu.CompilerParams(vmem_limit_bytes=GRANT),
+    )(enc_held, dec_held, grads, inputs, residual_grad, enc_bias.reshape(CHUNKS, 1, chunk), dec_bias.reshape(1, width))
+    return (enc_new, enc_bias.reshape(local), dec_new.T, dec_bias.reshape(width))
 
 
 def solution(mesh):

time: 180 us -> 157 us (0.87)
  local copies, waits for them, and re-layouts: 18.3 us -> 1.27 us
  Pallas kernels: 158 us -> 153 us
    unnamed x10 -> x0, local copies, waits for them, and re-layouts: 14.9 us -> none
    pallas_call x2 -> x1, Pallas kernels: 20.9 us -> 17.7 us  [fast_body(): pl.pallas_call(write_kernel, out_shape=(jax.ShapeDtypeStruct((width, loca...]
    pallas_call x2 -> x0, local copies, waits for them, and re-layouts: 2.1 us -> none  [fast_body(): pl.pallas_call(functools.partial(train_kernel, n_latent, n_rows, chunk),...]
    sub x2 -> x0, other arithmetic: 1.93 us -> none  [the longest x1 1.29 us: fast_body(): dec_bias - dec_bias_rate * jnp.sum(residual_grad, axis=0, dtype=F32)]
where the time goes in v1:
time: 157 us; the launch traced here: 156 us
  Pallas kernels  153 us (97%)
    pallas_call x1, Pallas kernels, fast_body(): pl.pallas_call(functools.partial(train_kernel, n_latent, n_rows, chunk),...  136 us
    pallas_call x1, Pallas kernels, fast_body(): pl.pallas_call(write_kernel, out_shape=(jax.ShapeDtypeStruct((width, loca...  17.7 us

profile of v1, /device:TPU:3, one launch (start us, length us, event | category | flops | bytes accessed | tf_op | source)
XLA Modules:
  0.0 156.4 jit_solution(1580965139562788119)
XLA Ops:
  0.6 1.3 reshape.27.dec_bias_ref
  1.9 135.6 %shard_map.111 = (bf16[8,576,2048]{2,1,0:T(8,128)(2,1)S(1)}, bf16[8,576,2048]{2,1,0:T(8,128)(2,1)S(1)}, bf16[16,64,2048]{2,1,0:T(8,128)(2,1)S(1)}, bf16[2,64,576...) custom-call(bf16[576,128]{1,0:T(8,128)(2,1)} %bitcast.12, bf16[576,1152]{1,0:T(8,128)(2,1)} %gate_ref.1, ...), custom_call_target="tpu_custom_call" | custom-call | tf_op jit(solution)/shard_map/pallas_call | solution.py:546
  137.5 17.7 %shard_map.112 = (bf16[576,16384]{1,0:T(8,128)(2,1)}, bf16[576,16384]{1,0:T(8,128)(2,1)}, f32[8,1,2048]{2,1,0:T(1,128)}, f32[1,576]{1,0:T(1,128)}) custom-call(bf16[8,576,2048]{2,1,0:T(8,128)(2,1)S(1)} %get-tuple-element.13.enc, bf16[8,576,2048]{2,1,0:T(8,128)(2,1)S(1)} %get-tuple-element.14.dec, bf16[16,64,2048]{2,1,0:T(8,128)(2,1)S(1)} %get-tuple-element.15.grads, ...), custom_call_target="tpu_custom_call" | custom-call | tf_op jit(solution)/shard_map/pallas_call | solution.py:602
  155.2 1.3 reduce

commit v2 on v1

--- a/solution.py
+++ b/solution.py
@@ -21,6 +21,7 @@
 F32 = jnp.float32
 CHUNKS = 8
 TILE = 256
+WIDE = 1024
 GRANT = 23 << 20
 
 
@@ -198,6 +199,7 @@
 HALVES = 2
 LEAD = 3
 RING = 4
+STAGED = 4
 
 
 def softplus(v):
@@ -228,7 +230,7 @@
     half = act.shape[1]
     own = half // 2
     small = half // n_latent
-    _, local_hidden = gate_ref.shape
+    width, local_hidden = gate_ref.shape
     count = enc.shape[0]
     items = HALVES * count
     mine = pl.ds(pl.multiple_of(core * own, own), own)
@@ -434,7 +436,7 @@
         for s, copy in enumerate(z_copies(2, h)):
             copy.wait_recv()
             total = total + resid_got[h, s]
-        grad = 2.0 * (dec_scale * total + dec_bias_ref[...] - share[h].astype(F32))
+        grad = 2.0 * (dec_scale * total + dec_bias_ref[...].reshape(1, width) - share[h].astype(F32))
         resid_share[h] = grad.astype(BF16)
         resid[h, my_small] = grad.astype(BF16)
         for copy in z_copies(3, h):
@@ -502,32 +504,32 @@
         span = slice(c * chunk, (c + 1) * chunk)
         return (
             pltpu.make_async_copy(dec.at[c], dec_out.at[:, span], dec_sem.at[c]),
-            pltpu.make_async_copy(staged.at[c % RING], enc_out.at[:, span], enc_sem.at[c]),
+            pltpu.make_async_copy(staged.at[c % STAGED], enc_out.at[:, span], enc_sem.at[c]),
         )
 
     copies = [out_copies(c) for c in range(count)]
     turned[...] = jnp.concatenate([features[h] for h in range(HALVES)], axis=0).T
     for c in range(count):
         copies[c][0].start()
-        if c >= RING:
-            copies[c - RING][1].wait()
+        if c >= STAGED:
+            copies[c - STAGED][1].wait()
 
         def tile_step(t, carry):
-            span = pl.ds(pl.multiple_of(t * TILE, TILE), TILE)
+            span = pl.ds(pl.multiple_of(t * WIDE, WIDE), WIDE)
             right = jnp.concatenate([grads[h * count + c, :, span] for h in range(HALVES)], axis=0)
             grad = jnp.dot(turned[...], right, preferred_element_type=F32)
-            staged[c % RING, :, span] = (enc[c, :, span].astype(F32) - enc_rate * grad).astype(BF16)
+            staged[c % STAGED, :, span] = (enc[c, :, span].astype(F32) - enc_rate * grad).astype(BF16)
             total = jnp.sum(right.astype(F32), axis=0, keepdims=True)
             bias_out[c, :, span] = bias_ref[c, :, span] - enc_bias_rate * total
             return carry
 
-        lax.fori_loop(0, chunk // TILE, tile_step, 0)
+        lax.fori_loop(0, chunk // WIDE, tile_step, 0)
         copies[c][1].start()
-    total = sum(jnp.sum(resid[h].astype(F32), axis=0, keepdims=True) for h in range(HALVES))
+    total = sum(jnp.sum(resid[h].astype(F32), axis=0) for h in range(HALVES))
     dec_bias_out[...] = dec_bias_ref[...] - dec_bias_rate * total
     for c in range(count):
         copies[c][0].wait()
-        if c >= count - RING:
+        if c >= count - STAGED:
             copies[c][1].wait()
 
 
@@ -594,7 +596,7 @@
         compiler_params=pltpu.CompilerParams(collective_id=0, has_side_effects=True, vmem_limit_bytes=GRANT),
     )(
         activations_in.reshape(tokens, activations_in.shape[2]).T, gate_proj, up_proj, down_proj.T, enc_weight,
-        enc_bias.reshape(CHUNKS, 1, chunk), dec_turned, dec_bias.reshape(1, width),
+        enc_bias.reshape(CHUNKS, 1, chunk), dec_turned, dec_bias,
     )
     enc_held, dec_held, grads, inputs, residual_grad = (
         pltpu.with_memory_space_constraint(v, vmem) for v in (enc_held, dec_held, grads, inputs, residual_grad)
@@ -605,19 +607,19 @@
             jax.ShapeDtypeStruct((width, local), BF16),
             jax.ShapeDtypeStruct((width, local), BF16),
             jax.ShapeDtypeStruct((CHUNKS, 1, chunk), F32),
-            jax.ShapeDtypeStruct((1, width), F32),
+            jax.ShapeDtypeStruct((width,), F32),
         ),
         in_specs=[vmem_spec] * 7,
         out_specs=(any_spec, any_spec, vmem_spec, vmem_spec),
         scratch_shapes=[
             vmem((width, tokens), BF16),
-            vmem((RING, width, chunk), BF16),
+            vmem((STAGED, width, chunk), BF16),
             dma((CHUNKS,)),
             dma((CHUNKS,)),
         ],
         compiler_params=pltpu.CompilerParams(vmem_limit_bytes=GRANT),
-    )(enc_held, dec_held, grads, inputs, residual_grad, enc_bias.reshape(CHUNKS, 1, chunk), dec_bias.reshape(1, width))
-    return (enc_new, enc_bias.reshape(local), dec_new.T, dec_bias.reshape(width))
+    )(enc_held, dec_held, grads, inputs, residual_grad, enc_bias.reshape(CHUNKS, 1, chunk), dec_bias)
+    return (enc_new, enc_bias.reshape(local), dec_new.T, dec_bias)
 
 
 def solution(mesh):

time: 157 us -> 150 us (0.955)
  Pallas kernels: 153 us -> 149 us
    pallas_call x1, Pallas kernels: 17.7 us -> 13.8 us  [fast_body(): pl.pallas_call(write_kernel, out_shape=(jax.ShapeDtypeStruct((width, loca...]
where the time goes in v2:
time: 150 us
  Pallas kernels  149 us (99%)
    pallas_call x1, Pallas kernels, fast_body(): pl.pallas_call(functools.partial(train_kernel, n_latent, n_rows, chunk),...  136 us
    pallas_call x1, Pallas kernels, fast_body(): pl.pallas_call(write_kernel, out_shape=(jax.ShapeDtypeStruct((width, loca...  13.8 us

profile of v2, /device:TPU:3, one launch (start us, length us, event | category | flops | bytes accessed | tf_op | source)
XLA Modules:
  0.0 150.2 jit_solution(17122505106697614072)
XLA Ops:
  0.6 135.6 %shard_map.111 = (bf16[8,576,2048]{2,1,0:T(8,128)(2,1)S(1)}, bf16[8,576,2048]{2,1,0:T(8,128)(2,1)S(1)}, bf16[16,64,2048]{2,1,0:T(8,128)(2,1)S(1)}, bf16[2,64,576...) custom-call(bf16[576,128]{1,0:T(8,128)(2,1)} %bitcast.12, bf16[576,1152]{1,0:T(8,128)(2,1)} %gate_ref.1, ...), custom_call_target="tpu_custom_call" | custom-call | tf_op jit(solution)/shard_map/pallas_call | solution.py:548
  136.2 13.8 %shard_map.112 = (bf16[576,16384]{1,0:T(8,128)(2,1)}, bf16[576,16384]{1,0:T(8,128)(2,1)}, f32[8,1,2048]{2,1,0:T(1,128)}, f32[576]{0:T(1024)}) custom-call(bf16[8,576,2048]{2,1,0:T(8,128)(2,1)S(1)} %get-tuple-element.13.enc, bf16[8,576,2048]{2,1,0:T(8,128)(2,1)S(1)} %get-tuple-element.14.dec, bf16[16,64,2048]{2,1,0:T(8,128)(2,1)S(1)} %get-tuple-element.15.grads, ...), custom_call_target="tpu_custom_call" | custom-call | tf_op jit(solution)/shard_map/pallas_call | solution.py:604

commit v3 on v2

--- a/solution.py
+++ b/solution.py
@@ -256,8 +256,6 @@
         span = slice(c * chunk, (c + 1) * chunk)
         weights.append(pltpu.make_async_copy(enc_ref.at[:, span], enc.at[c], weight_sem.at[0, c]))
         weights.append(pltpu.make_async_copy(dec_ref.at[:, span], dec.at[c], weight_sem.at[1, c]))
-    for load in weights:
-        load.start()
 
     barrier = pltpu.get_barrier_semaphore()
     for to in [mate, far] + others:
@@ -279,12 +277,15 @@
         for h in range(HALVES):
             act[h] = act_own[h]
 
+    for load in loads[1:]:
+        load.wait()
+    for load in weights:
+        load.start()
+
     @pl.when(z != rows)
     def _():
         act_copy(0, 0).wait_recv()
 
-    loads[1].wait()
-    loads[2].wait()
 
     def ffn_copy(stage, h):
         src, dst, to = (
@@ -314,7 +315,6 @@
                 act_copy(h, 0).wait_recv()
         ffn_part[h] = jnp.dot(act[h], gate_up[...], preferred_element_type=F32).astype(BF16)
         ffn_copy(0, h).start()
-    for h in range(HALVES):
         ffn_copy(0, h).wait_recv()
         ffn_sum[h] = (ffn_part[h, mine].astype(F32) + ffn_got[h].astype(F32)).astype(BF16)
         ffn_copy(1, h).start()
@@ -324,8 +324,6 @@
         gate_term, up_term = total[:, :local_hidden], total[:, local_hidden:]
         hidden[h, mine] = (jax.nn.gelu(gate_term, approximate=True) * up_term).astype(BF16)
         ffn_copy(2, h).start()
-    loads[3].wait()
-    for h in range(HALVES):
         ffn_copy(2, h).wait_recv()
         part_value = over_last(hidden[h], down[...])
         acc[h] = part_value

time: 150 us -> 140 us (0.933)
  Pallas kernels: 149 us -> 139 us
    pallas_call x1, Pallas kernels: 136 us -> 126 us  [fast_body(): pl.pallas_call(functools.partial(train_kernel, n_latent, n_rows, chunk),...]
where the time goes in v3:
time: 140 us
  Pallas kernels  139 us (99%)
    pallas_call x1, Pallas kernels, fast_body(): pl.pallas_call(functools.partial(train_kernel, n_latent, n_rows, chunk),...  126 us
    pallas_call x1, Pallas kernels, fast_body(): pl.pallas_call(write_kernel, out_shape=(jax.ShapeDtypeStruct((width, loca...  13.8 us

profile of v3, /device:TPU:3, one launch (start us, length us, event | category | flops | bytes accessed | tf_op | source)
XLA Modules:
  0.0 140.2 jit_solution(6374654000577426123)
XLA Ops:
  0.6 125.6 %shard_map.111 = (bf16[8,576,2048]{2,1,0:T(8,128)(2,1)S(1)}, bf16[8,576,2048]{2,1,0:T(8,128)(2,1)S(1)}, bf16[16,64,2048]{2,1,0:T(8,128)(2,1)S(1)}, bf16[2,64,576...) custom-call(bf16[576,128]{1,0:T(8,128)(2,1)} %bitcast.12, bf16[576,1152]{1,0:T(8,128)(2,1)} %gate_ref.1, ...), custom_call_target="tpu_custom_call" | custom-call | tf_op jit(solution)/shard_map/pallas_call | solution.py:546
  126.2 13.8 %shard_map.112 = (bf16[576,16384]{1,0:T(8,128)(2,1)}, bf16[576,16384]{1,0:T(8,128)(2,1)}, f32[8,1,2048]{2,1,0:T(1,128)}, f32[576]{0:T(1024)}) custom-call(bf16[8,576,2048]{2,1,0:T(8,128)(2,1)S(1)} %get-tuple-element.13.enc, bf16[8,576,2048]{2,1,0:T(8,128)(2,1)S(1)} %get-tuple-element.14.dec, bf16[16,64,2048]{2,1,0:T(8,128)(2,1)S(1)} %get-tuple-element.15.grads, ...), custom_call_target="tpu_custom_call" | custom-call | tf_op jit(solution)/shard_map/pallas_call | solution.py:602
